TPU v7x, 32 devices: a whole 2x2x4 slice. The times are simulated.
32 devices in a mesh: dp: 8 (over z, x), tensor: 4 (over y, core).
Axes of the slice: x: 2, y: 2, z: 4, core: 2. Of those that a mesh axis runs over, the one named last changes fastest.
Arguments:
- tokens: bfloat16 [16384, 768], P('dp'), may hold values from -6 to 6
- seq_lens: int32 [16], P('dp'), may hold values from 512 to 1024, as said below
- block_sizes: int32 [16], P('dp'), may hold values from 128 to 512
- w_query: bfloat16 [768, 768], P('dp', 'tensor'), may hold values from -0.3125 to 0.3125
- b_query: bfloat16 [768], P('tensor'), may hold values from -3 to 3
- w_key: bfloat16 [768, 768], P('dp', 'tensor'), may hold values from -0.21875 to 0.21875
- w_value: bfloat16 [768, 768], P('dp', 'tensor'), may hold values from -0.21875 to 0.21875
- b_value: bfloat16 [768], P('tensor'), may hold values from -3 to 3
- w_out: bfloat16 [768, 768], P('tensor', 'dp'), may hold values from -1.25 to 1.25
- b_out: bfloat16 [768], P('dp'), may hold values from -2 to 2
- gain_one: bfloat16 [768], P('dp'), may hold values from 0.25 to 1.75
- shift_one: bfloat16 [768], P('dp'), may hold values from -2 to 2
- w_up: bfloat16 [768, 3072], P('dp', 'tensor'), may hold values from -0.21875 to 0.21875
- b_up: bfloat16 [3072], P('tensor'), may hold values from -3 to 3
- w_down: bfloat16 [3072, 768], P('tensor', 'dp'), may hold values from -0.109375 to 0.109375
- b_down: bfloat16 [768], P('dp'), may hold values from -2 to 2
- gain_two: bfloat16 [768], P('dp'), may hold values from 0.25 to 1.75
- shift_two: bfloat16 [768], P('dp'), may hold values from -2 to 2
- cotangent: bfloat16 [16384, 768], P('dp'), may hold values from -6 to 6
Outputs:
- output: bfloat16 [16384, 768], P('dp')
- input_grad: float32 [16384, 768], P('dp', 'tensor')
- grad_w_query: float32 [768, 768], P('dp', 'tensor')
- grad_b_query: float32 [768], P('tensor')
- grad_w_key: float32 [768, 768], P('dp', 'tensor')
- grad_w_value: float32 [768, 768], P('dp', 'tensor')
- grad_b_value: float32 [768], P('tensor')
- grad_w_out: float32 [768, 768], P('tensor', 'dp')
- grad_b_out: float32 [768], P('dp')
- grad_gain_one: float32 [768], P('dp')
- grad_shift_one: float32 [768], P('dp')
- grad_w_up: float32 [768, 3072], P('dp', 'tensor')
- grad_b_up: float32 [3072], P('tensor')
- grad_w_down: float32 [3072, 768], P('tensor', 'dp')
- grad_b_down: float32 [768], P('dp')
- grad_gain_two: float32 [768], P('dp')
- grad_shift_two: float32 [768], P('dp')
Inputs may be any that keep to these rules, and one draw needn't show every extreme that they name: seq_lens[s] counts the key positions of sequence s that any query may see; at least one sequence is whole.
All inputs are finite; a program needn't handle non-finite values.
Results may differ from a plain program's by a relative error of at most 0.015.
The roundings to bfloat16 on the way count: a program that leaves them out, or rounds other values in their place, can miss the bound.
Values may be sent and summed in bfloat16 or wider, within the bound.
A program may use at most 192 MiB of HBM per device.

v0:
```python
import jax
import jax.numpy as jnp
from jax import lax
from jax.sharding import PartitionSpec as P

HEAD = 64
norm_epsilon = 1e-12
inv_root_two = 0.7071067811865476
inv_root_tau = 0.3989422804014327
masked_score = -1000000000.0


def matmul(first_operand, second_operand):
    return jnp.dot(first_operand, second_operand, preferred_element_type=jnp.float32)


def contract_rows(first_operand, second_operand):
    return lax.dot_general(
        first_operand, second_operand, (((0,), (0,)), ((), ())), preferred_element_type=jnp.float32
    )


def contract_cols(first_operand, second_operand):
    return lax.dot_general(
        first_operand, second_operand, (((1,), (1,)), ((), ())), preferred_element_type=jnp.float32
    )


def norm_forward(row_values, gain_row, offset_row):
    row_mean = jnp.mean(row_values, axis=-1, keepdims=True)
    centred = row_values - row_mean
    variance = jnp.mean(centred * centred, axis=-1, keepdims=True)
    inv_scale = lax.rsqrt(variance + norm_epsilon)
    normal_rows = centred * inv_scale
    return (normal_rows * gain_row + offset_row, normal_rows, inv_scale)


def norm_backward(upstream, normal_rows, inv_scale, gain_row):
    scaled = upstream * gain_row
    row_grad = inv_scale * (
        scaled
        - jnp.mean(scaled, axis=-1, keepdims=True)
        - normal_rows * jnp.mean(scaled * normal_rows, axis=-1, keepdims=True)
    )
    return (row_grad, jnp.sum(upstream * normal_rows, axis=0), jnp.sum(upstream, axis=0))


def allowed_mask(first_row, row_total, key_total, seq_length, block_size):
    row_pos = first_row + lax.broadcasted_iota(jnp.int32, (row_total, key_total), 0)
    key_pos = lax.broadcasted_iota(jnp.int32, (row_total, key_total), 1)
    return (key_pos // block_size <= row_pos // block_size) & (key_pos < seq_length)


def attend(query_rows, key_rows, value_rows, seq_length, block_size):
    row_total, local_heads, head_size = query_rows.shape
    block_rows = min(512, row_total)
    block_count = row_total // block_rows
    query_blocks = query_rows.reshape(block_count, block_rows, local_heads, head_size)

    def one_block(block_pair):
        block_index, query_block = block_pair
        scores = jnp.einsum(
            "qhd,khd->hqk", query_block, key_rows, preferred_element_type=jnp.float32
        )
        allowed = allowed_mask(
            block_index * block_rows, block_rows, row_total, seq_length, block_size
        )
        scores = jnp.where(allowed[None], scores, masked_score)
        top_score = jnp.max(scores, axis=-1, keepdims=True)
        exp_scores = jnp.exp(scores - top_score)
        exp_total = jnp.sum(exp_scores, axis=-1, keepdims=True)
        probabilities = (exp_scores / exp_total).astype(jnp.bfloat16)
        context = jnp.einsum(
            "hqk,khd->qhd", probabilities, value_rows, preferred_element_type=jnp.float32
        )
        return (context.astype(jnp.bfloat16), top_score[..., 0] + jnp.log(exp_total[..., 0]))

    contexts, log_sums = lax.map(
        one_block, (jnp.arange(block_count, dtype=jnp.int32), query_blocks)
    )
    return (contexts.reshape(row_total, local_heads * head_size), log_sums)


def attend_back(query_rows, key_rows, value_rows, context_grad, log_sums, seq_length, block_size):
    row_total, local_heads, head_size = query_rows.shape
    block_rows = min(512, row_total)
    block_count = row_total // block_rows
    query_blocks = query_rows.reshape(block_count, block_rows, local_heads, head_size)
    grad_blocks = context_grad.reshape(block_count, block_rows, local_heads, head_size)

    def one_block(running, block_pack):
        key_grad, value_grad = running
        block_index, query_block, grad_block, log_block = block_pack
        scores = jnp.einsum(
            "qhd,khd->hqk", query_block, key_rows, preferred_element_type=jnp.float32
        )
        allowed = allowed_mask(
            block_index * block_rows, block_rows, row_total, seq_length, block_size
        )
        probabilities = jnp.where(allowed[None], jnp.exp(scores - log_block[..., None]), 0.0)
        prob_grad = jnp.einsum(
            "qhd,khd->hqk", grad_block, value_rows, preferred_element_type=jnp.float32
        )
        row_dot = jnp.sum(prob_grad * probabilities, axis=-1, keepdims=True)
        score_grad = (probabilities * (prob_grad - row_dot)).astype(jnp.bfloat16)
        query_grad = jnp.einsum(
            "hqk,khd->qhd", score_grad, key_rows, preferred_element_type=jnp.float32
        )
        key_grad = key_grad + jnp.einsum(
            "hqk,qhd->khd", score_grad, query_block, preferred_element_type=jnp.float32
        )
        value_grad = value_grad + jnp.einsum(
            "hqk,qhd->khd",
            probabilities.astype(jnp.bfloat16),
            grad_block,
            preferred_element_type=jnp.float32,
        )
        return ((key_grad, value_grad), query_grad)

    empty = jnp.zeros((row_total, local_heads, head_size), jnp.float32)
    (key_grad, value_grad), query_grads = lax.scan(
        one_block,
        (empty, empty),
        (jnp.arange(block_count, dtype=jnp.int32), query_blocks, grad_blocks, log_sums),
    )
    width = local_heads * head_size
    return (
        query_grads.reshape(row_total, width),
        key_grad.reshape(row_total, width),
        value_grad.reshape(row_total, width),
    )


def on_device(
    tokens,
    seq_lens,
    block_sizes,
    w_query,
    b_query,
    w_key,
    w_value,
    b_value,
    w_out,
    b_out,
    gain_one,
    shift_one,
    w_up,
    b_up,
    w_down,
    b_down,
    gain_two,
    shift_two,
    cotangent,
):
    micro_total = seq_lens.shape[0]
    seq_rows = tokens.shape[0] // micro_total
    head_cols = w_query.shape[1]
    local_heads = head_cols // HEAD
    model_width = tokens.shape[1]
    own_cols = model_width // lax.axis_size("tensor")
    column_start = lax.axis_index("tensor") * own_cols
    query_bias = b_query.astype(jnp.float32)
    value_bias = b_value.astype(jnp.float32)
    up_bias = b_up.astype(jnp.float32)
    owned = (
        w_query,
        w_key,
        w_value,
        w_out,
        w_up,
        w_down,
        b_out,
        gain_one,
        shift_one,
        b_down,
        gain_two,
        shift_two,
    )

    def shaped(flat_rows):
        return flat_rows.reshape(seq_rows, local_heads, HEAD)

    layer_outputs = []
    input_grads = []
    totals = None
    for micro_index in range(micro_total):
        rows_in = tokens[micro_index * seq_rows : (micro_index + 1) * seq_rows]
        upstream = cotangent[micro_index * seq_rows : (micro_index + 1) * seq_rows].astype(
            jnp.float32
        )
        seq_length = seq_lens[micro_index]
        block_size = block_sizes[micro_index]
        forward_set = (
            lax.all_gather(owned[0], "dp", axis=0, tiled=True),
            lax.all_gather(owned[1], "dp", axis=0, tiled=True),
            lax.all_gather(owned[2], "dp", axis=0, tiled=True),
            lax.all_gather(owned[3], "dp", axis=1, tiled=True),
            lax.all_gather(owned[4], "dp", axis=0, tiled=True),
            lax.all_gather(owned[5], "dp", axis=1, tiled=True),
            lax.all_gather(owned[6], "dp", axis=0, tiled=True),
            lax.all_gather(owned[7], "dp", axis=0, tiled=True),
            lax.all_gather(owned[8], "dp", axis=0, tiled=True),
            lax.all_gather(owned[9], "dp", axis=0, tiled=True),
            lax.all_gather(owned[10], "dp", axis=0, tiled=True),
            lax.all_gather(owned[11], "dp", axis=0, tiled=True),
        )
        (
            full_query,
            full_key,
            full_value,
            full_out,
            full_up,
            full_down,
            full_out_bias,
            full_gain_one,
            full_shift_one,
            full_down_bias,
            full_gain_two,
            full_shift_two,
        ) = forward_set
        out_bias = full_out_bias.astype(jnp.float32)
        down_bias = full_down_bias.astype(jnp.float32)
        first_gain = full_gain_one.astype(jnp.float32)
        first_shift = full_shift_one.astype(jnp.float32)
        second_gain = full_gain_two.astype(jnp.float32)
        second_shift = full_shift_two.astype(jnp.float32)
        query_rows = ((matmul(rows_in, full_query) + query_bias) * 0.125).astype(jnp.bfloat16)
        key_rows = matmul(rows_in, full_key).astype(jnp.bfloat16)
        value_rows = (matmul(rows_in, full_value) + value_bias).astype(jnp.bfloat16)
        context, log_sums = attend(
            shaped(query_rows), shaped(key_rows), shaped(value_rows), seq_length, block_size
        )
        attended = lax.psum(matmul(context, full_out), "tensor") + out_bias
        first_norm, first_hat, first_scale = norm_forward(
            rows_in.astype(jnp.float32) + attended, first_gain, first_shift
        )
        normed = first_norm.astype(jnp.bfloat16)
        expanded = matmul(normed, full_up) + up_bias
        normal_cdf = 0.5 * (1.0 + lax.erf(expanded * inv_root_two))
        hidden = (expanded * normal_cdf).astype(jnp.bfloat16)
        lowered = lax.psum(matmul(hidden, full_down), "tensor") + down_bias
        second_norm, second_hat, second_scale = norm_forward(
            normed.astype(jnp.float32) + lowered, second_gain, second_shift
        )
        layer_outputs.append(second_norm.astype(jnp.bfloat16))
        second_grad, grad_gain_two, grad_shift_two = norm_backward(
            upstream, second_hat, second_scale, second_gain
        )
        down_bias_grad = jnp.sum(second_grad, axis=0)
        second_low = second_grad.astype(jnp.bfloat16)
        down_grad = contract_rows(hidden, second_low)
        hidden_grad = contract_cols(second_low, full_down)
        expanded_grad = hidden_grad * (
            normal_cdf + expanded * jnp.exp(-0.5 * expanded * expanded) * inv_root_tau
        )
        up_bias_grad = jnp.sum(expanded_grad, axis=0)
        expanded_low = expanded_grad.astype(jnp.bfloat16)
        up_grad = contract_rows(normed, expanded_low)
        normed_grad = lax.psum(contract_cols(expanded_low, full_up), "tensor") + second_grad
        first_grad, grad_gain_one, grad_shift_one = norm_backward(
            normed_grad, first_hat, first_scale, first_gain
        )
        out_bias_grad = jnp.sum(first_grad, axis=0)
        first_low = first_grad.astype(jnp.bfloat16)
        out_grad = contract_rows(context, first_low)
        context_grad = contract_cols(first_low, full_out).astype(jnp.bfloat16)
        query_grad, key_grad, value_grad = attend_back(
            shaped(query_rows),
            shaped(key_rows),
            shaped(value_rows),
            shaped(context_grad),
            log_sums,
            seq_length,
            block_size,
        )
        query_grad = query_grad * 0.125
        query_bias_grad = jnp.sum(query_grad, axis=0)
        value_bias_grad = jnp.sum(value_grad, axis=0)
        query_low = query_grad.astype(jnp.bfloat16)
        key_low = key_grad.astype(jnp.bfloat16)
        value_low = value_grad.astype(jnp.bfloat16)
        query_w_grad = contract_rows(rows_in, query_low)
        key_w_grad = contract_rows(rows_in, key_low)
        value_w_grad = contract_rows(rows_in, value_low)
        input_term = (
            contract_cols(query_low, full_query)
            + contract_cols(key_low, full_key)
            + contract_cols(value_low, full_value)
        )
        own_grad = lax.psum_scatter(
            input_term.astype(jnp.bfloat16), "tensor", scatter_dimension=1, tiled=True
        ).astype(jnp.float32)
        input_grads.append(
            own_grad + lax.dynamic_slice_in_dim(first_grad, column_start, own_cols, 1)
        )
        terms = (
            query_w_grad,
            query_bias_grad,
            key_w_grad,
            value_w_grad,
            value_bias_grad,
            out_grad,
            out_bias_grad,
            grad_gain_one,
            grad_shift_one,
            up_grad,
            up_bias_grad,
            down_grad,
            down_bias_grad,
            grad_gain_two,
            grad_shift_two,
        )
        if totals is None:
            totals = terms
        else:
            totals = tuple((running + addend for running, addend in zip(totals, terms)))
    summed = (
        lax.psum_scatter(totals[0], "dp", scatter_dimension=0, tiled=True),
        lax.psum_scatter(totals[2], "dp", scatter_dimension=0, tiled=True),
        lax.psum_scatter(totals[3], "dp", scatter_dimension=0, tiled=True),
        lax.psum_scatter(totals[5], "dp", scatter_dimension=1, tiled=True),
        lax.psum_scatter(totals[9], "dp", scatter_dimension=0, tiled=True),
        lax.psum_scatter(totals[11], "dp", scatter_dimension=1, tiled=True),
        lax.psum_scatter(totals[6], "dp", scatter_dimension=0, tiled=True),
        lax.psum_scatter(totals[7], "dp", scatter_dimension=0, tiled=True),
        lax.psum_scatter(totals[8], "dp", scatter_dimension=0, tiled=True),
        lax.psum_scatter(totals[12], "dp", scatter_dimension=0, tiled=True),
        lax.psum_scatter(totals[13], "dp", scatter_dimension=0, tiled=True),
        lax.psum_scatter(totals[14], "dp", scatter_dimension=0, tiled=True),
    )
    bias_sums = lax.psum((totals[1], totals[4], totals[10]), "dp")
    return (
        jnp.concatenate(layer_outputs, 0),
        jnp.concatenate(input_grads, 0),
        summed[0],
        bias_sums[0],
        summed[1],
        summed[2],
        bias_sums[1],
        summed[3],
        summed[6],
        summed[7],
        summed[8],
        summed[4],
        bias_sums[2],
        summed[5],
        summed[9],
        summed[10],
        summed[11],
    )


def solution(mesh):
    in_specs = (
        P("dp", None),
        P("dp"),
        P("dp"),
        P("dp", "tensor"),
        P("tensor"),
        P("dp", "tensor"),
        P("dp", "tensor"),
        P("tensor"),
        P("tensor", "dp"),
        P("dp"),
        P("dp"),
        P("dp"),
        P("dp", "tensor"),
        P("tensor"),
        P("tensor", "dp"),
        P("dp"),
        P("dp"),
        P("dp"),
        P("dp", None),
    )
    out_specs = (
        P("dp", None),
        P("dp", "tensor"),
        P("dp", "tensor"),
        P("tensor"),
        P("dp", "tensor"),
        P("dp", "tensor"),
        P("tensor"),
        P("tensor", "dp"),
        P("dp"),
        P("dp"),
        P("dp"),
        P("dp", "tensor"),
        P("tensor"),
        P("tensor", "dp"),
        P("dp"),
        P("dp"),
        P("dp"),
    )
    return jax.shard_map(
        on_device, mesh=mesh, in_specs=in_specs, out_specs=out_specs, check_vma=False
    )
```

profile of v0, /device:TPU:0, one launch (start us, length us, event | category | flops | bytes accessed | tf_op | source)
XLA Modules:
  0.0 1132.8 jit_solution(600460367562046693)
XLA Ops:
  8.1 33.1 %all_gather.48 = bf16[768,192]{1,0:T(8,128)(2,1)S(1)} all-gather(bf16[96,192]{1,0:T(8,128)(2,1)} %param.30), channel_id=1, replica_groups=mesh['dp'=8,'tensor'=4] {'dp'}, dimensions={0}, use_global_device_ids=true | all-gather | bytes 331776 | tf_op jit(solution)/shard_map/all_gather | solution.py:194
  46.2 31.1 %all_gather.50 = bf16[768,192]{1,0:T(8,128)(2,1)S(1)} all-gather(bf16[96,192]{1,0:T(8,128)(2,1)S(1)} %copy-done.68), channel_id=1, replica_groups=mesh['dp'=8,'tensor'=4] {'dp'}, dimensions={0}, use_global_device_ids=true | all-gather | bytes 331776 | tf_op jit(solution)/shard_map/all_gather | solution.py:196
  79.4 31.1 %all_gather.49 = bf16[768,192]{1,0:T(8,128)(2,1)S(1)} all-gather(bf16[96,192]{1,0:T(8,128)(2,1)S(1)} %copy-done.69), channel_id=1, replica_groups=mesh['dp'=8,'tensor'=4] {'dp'}, dimensions={0}, use_global_device_ids=true | all-gather | bytes 331776 | tf_op jit(solution)/shard_map/all_gather | solution.py:195
  114.2 21.0 %while.66 = (s32[]{:T(128)}, bf16[2,512,3,64]{1,3,2,0:T(8,128)(2,1)S(1)}, f32[2,3,512]{2,1,0:T(4,128)S(1)}, s32[]{:T(128)}, s32[]{:T(128)}, /*index=5*/s32[2]{0:...) while((s32[]{:T(128)}, ...), condition=%wide.region_3.4_spmd, body=%wide.region_0.3_spmd.sunk | while | flops 419015680 | bytes 22240444 | solution.py:78
  135.8 31.2 %all_gather.51 = bf16[192,768]{0,1:T(8,128)(2,1)S(1)} all-gather(bf16[192,96]{0,1:T(8,128)(2,1)S(1)} %copy.74), channel_id=1, replica_groups=mesh['dp'=8,'tensor'=4] {'dp'}, dimensions={1}, use_global_device_ids=true | all-gather | bytes 331776 | tf_op jit(solution)/shard_map/all_gather | solution.py:197
  168.0 21.0 %while.67 = (s32[]{:T(128)}, bf16[2,512,3,64]{1,3,2,0:T(8,128)(2,1)S(1)}, f32[2,3,512]{2,1,0:T(4,128)S(1)}, s32[]{:T(128)}, s32[]{:T(128)}, /*index=5*/s32[2]{0:...) while((s32[]{:T(128)}, ...), condition=%wide.region_13.14_spmd, body=%wide.region_10.13_spmd.sunk | while | flops 419015680 | bytes 22240444 | solution.py:78
  198.3 38.0 %all-reduce.16 = (bf16[768]{0:T(1024)(128)(2,1)S(1)}, bf16[768]{0:T(1024)(128)(2,1)S(1)}, bf16[768]{0:T(1024)(128)(2,1)S(1)}, bf16[768]{0:T(1024)(128)(2,1)S(1)}...) all-reduce(bf16[768]{0:T(1024)(128)(2,1)S(1)} %dynamic-update-slice, ...), channel_id=1, replica_groups=mesh['dp'=8,'tensor'=4] {'dp'}, use_global_device_ids=true, to_apply=%add | all-reduce | flops 4608 | bytes 18432
  236.4 78.9 %all-reduce.25.cloned.1.call-done = (f32[1024,768]{1,0:T(8,128)}, f32[1024,768]{1,0:T(8,128)}) async-done(((f32[1024,768]{1,0:T(8,128)}, f32[1024,768]{1,0:T(8,128)}), (f32[1024,768]{1,0:T(8,128)}, f32[1024,768]{1,0:T(8,128)})) %all-reduce.25.cloned.1.call-update) | async-done | bytes 6291472 | tf_op jit(solution)/shard_map/psum | solution.py:233
  315.4 4.7 fusion.169
  329.7 3.8 multiply_convert_fusion.3
  333.5 4.9 fusion.179
  342.1 119.6 %all-reduce.23.cloned.1.call-done = (f32[1024,768]{1,0:T(8,128)}, f32[1024,768]{1,0:T(8,128)}) async-done(((f32[1024,768]{1,0:T(8,128)}, f32[1024,768]{1,0:T(8,128)}), (f32[1024,768]{1,0:T(8,128)}, f32[1024,768]{1,0:T(8,128)})) %all-reduce.23.cloned.1.call-update) | async-done | bytes 6291472 | tf_op jit(solution)/shard_map/psum | solution.py:241
  461.7 4.2 fusion.167
  467.9 3.6 convert_reduce_fusion
  471.5 4.6 fusion.161
  489.7 119.9 %all-reduce.21.cloned.1.call-done = (f32[1024,768]{1,0:T(8,128)}, f32[1024,768]{1,0:T(8,128)}) async-done(((f32[1024,768]{1,0:T(8,128)}, f32[1024,768]{1,0:T(8,128)}), (f32[1024,768]{1,0:T(8,128)}, f32[1024,768]{1,0:T(8,128)})) %all-reduce.21.cloned.1.call-update) | async-done | bytes 6291472 | tf_op jit(solution)/shard_map/psum | solution.py:259
  609.6 5.4 multiply_reduce_fusion.3
  617.0 3.6 fusion.166
  628.8 44.0 %while.68 = (s32[]{:T(128)}, f32[1024,3,64]{0,2,1:T(8,128)}, f32[1024,3,64]{0,2,1:T(8,128)}, f32[2,512,3,64]{1,3,2,0:T(8,128)}, bf16[2,512,3,64]{1,3,2,0:T(8,128...) while((s32[]{:T(128)}, f32[1024,3,64]{0,2,1:T(8,128)}, ...), condition=%wide.region_27.28_spmd.clone, body=%wide.region_25.27_spmd.clone.sunk | while | flops 1028402176 | bytes 118828048 | solution.py:121
  636.0 3.6 multiply_reduce_fusion.16
  657.8 3.7 multiply_reduce_fusion.16
  669.1 3.7 fusion.327
  675.1 40.6 %while.69 = (s32[]{:T(128)}, f32[1024,3,64]{0,2,1:T(8,128)}, f32[1024,3,64]{0,2,1:T(8,128)}, f32[2,512,3,64]{1,3,2,0:T(8,128)}, bf16[2,512,3,64]{1,3,2,0:T(8,128...) while((s32[]{:T(128)}, f32[1024,3,64]{0,2,1:T(8,128)}, ...), condition=%wide.region_36.37_spmd.clone, body=%wide.region_34.36_spmd.clone.sunk | while | flops 1028402176 | bytes 114159056 | solution.py:121
  712.1 3.6 fusion.343
  743.9 4.0 fusion.143
  750.9 3.5 fusion.139
  761.0 37.7 %all-reduce.12 = (f32[192]{0:T(256)}, f32[192]{0:T(256)}, f32[768]{0:T(1024)S(1)}, f32[768]{0:T(1024)S(1)}, f32[768]{0:T(1024)S(1)}, /*index=5*/f32[768]{0:T(102...) all-reduce(f32[192]{0:T(256)S(1)} %add.515, ...), channel_id=1, replica_groups=mesh['dp'=8,'tensor'=4] {'dp'}, use_global_device_ids=true, to_apply=%region_41.42 | all-reduce | flops 5760 | bytes 46080 | tf_op jit(solution)/shard_map/psum | solution.py:331
  811.7 38.2 %reduce-scatter.33.cloned.1.call-done = f32[96,192]{1,0:T(8,128)} async-done(((f32[768,192]{1,0:T(8,128)}), f32[96,192]{1,0:T(8,128)}) %reduce-scatter.33.cloned.1.call-update) | async-done | bytes 73744
  850.0 65.4 %reduce-scatter.31.cloned.1.call-done = f32[96,192]{1,0:T(8,128)} async-done(((f32[768,192]{1,0:T(8,128)}), f32[96,192]{1,0:T(8,128)}) %reduce-scatter.31.cloned.1.call-update) | async-done | bytes 73744
  915.4 65.7 %reduce-scatter.29.cloned.1.call-done = f32[96,192]{1,0:T(8,128)} async-done(((f32[768,192]{1,0:T(8,128)}), f32[96,192]{1,0:T(8,128)}) %reduce-scatter.29.cloned.1.call-update) | async-done | bytes 73744
  981.1 72.0 %reduce-scatter.23.cloned.1.call-done = f32[768,96]{0,1:T(8,128)} async-done(((f32[768,768]{0,1:T(8,128)}), f32[768,96]{0,1:T(8,128)}) %reduce-scatter.23.cloned.1.call-update) | async-done | bytes 294928 | tf_op jit(solution)/shard_map/reduce_scatter | solution.py:323
  1053.1 72.1 %reduce-scatter.21.cloned.1.call-done = f32[96,768]{1,0:T(8,128)} async-done(((f32[768,768]{1,0:T(8,128)}), f32[96,768]{1,0:T(8,128)}) %reduce-scatter.21.cloned.1.call-update) | async-done | bytes 294928 | tf_op jit(solution)/shard_map/reduce_scatter | solution.py:322
  (513 shorter events, 215.6 us)
Async XLA Ops:
  8.0 36.7 %copy-start.23 = (bf16[2048,768]{1,0:T(8,128)(2,1)S(1)}, bf16[2048,768]{1,0:T(8,128)(2,1)}, u32[]{:S(2)}) copy-start(bf16[2048,768]{1,0:T(8,128)(2,1)} %param.27) | copy-start | bytes 9437188
  8.0 307.3 %all-reduce.25.cloned.1.call-start = ((), (), s32[]{:S(2)}) async-start(), calls=%async_computation.20 | async-start | bytes 12582912 | tf_op jit(solution)/shard_map/psum | solution.py:233
  41.9 35.4 %copy-start.93 = (bf16[192]{0:T(256)(128)(2,1)S(1)}, bf16[192]{0:T(256)(128)(2,1)}, u32[]{:S(2)}) copy-start(bf16[192]{0:T(256)(128)(2,1)} %param.34) | copy-start | bytes 1156
  46.2 33.2 %copy-start.69 = (bf16[96,192]{1,0:T(8,128)(2,1)S(1)}, bf16[96,192]{1,0:T(8,128)(2,1)}, u32[]{:S(2)}) copy-start(bf16[96,192]{1,0:T(8,128)(2,1)} %param.32) | copy-start | bytes 110596
  77.3 34.0 %copy-start.43 = (bf16[768,192]{1,0:T(8,128)(2,1)}, bf16[768,192]{1,0:T(8,128)(2,1)S(1)}, u32[]{:S(2)}) copy-start(bf16[768,192]{1,0:T(8,128)(2,1)S(1)} %all_gather.50) | copy-start | bytes 884740
  77.3 33.2 %copy-start.24 = (bf16[2048,768]{1,0:T(8,128)(2,1)S(1)}, bf16[2048,768]{1,0:T(8,128)(2,1)}, u32[]{:S(2)}) copy-start(bf16[2048,768]{1,0:T(8,128)(2,1)} %param.27) | copy-start | bytes 9437188
  79.4 32.5 %copy-start.64 = (bf16[1024,192]{0,1:T(8,128)(2,1)S(1)}, bf16[1024,192]{0,1:T(8,128)(2,1)}, u32[]{:S(2)}) copy-start(bf16[1024,192]{0,1:T(8,128)(2,1)} %fusion.122) | copy-start | bytes 1179652
  114.2 21.5 %copy-start.70 = (bf16[192,96]{1,0:T(8,128)(2,1)S(1)}, bf16[192,96]{1,0:T(8,128)(2,1)}, u32[]{:S(2)}) copy-start(bf16[192,96]{1,0:T(8,128)(2,1)} %param.35) | copy-start | bytes 110596
  114.2 52.8 %copy-start.63 = (bf16[1024,192]{0,1:T(8,128)(2,1)S(1)}, bf16[1024,192]{0,1:T(8,128)(2,1)}, u32[]{:S(2)}) copy-start(bf16[1024,192]{0,1:T(8,128)(2,1)} %fusion.123) | copy-start | bytes 1179652
  135.7 54.0 %copy-start.57 = (bf16[24,8,2,512]{3,1,2,0:T(8,128)(2,1)}, bf16[24,8,2,512]{3,1,2,0:T(8,128)(2,1)S(1)}, u32[]{:S(2)}) copy-start(bf16[24,8,2,512]{3,1,2,0:T(8,128)(2,1)S(1)} %copy.101) | copy-start | bytes 1179652
  194.4 42.0 %copy-start.85 = (bf16[768]{0:T(1024)(128)(2,1)S(1)}, bf16[768]{0:T(1024)(128)(2,1)}, u32[]{:S(2)}) copy-start(bf16[768]{0:T(1024)(128)(2,1)} %param.40) | copy-start | bytes 4612
  194.4 130.3 %all-gather.3.cloned.1.call-start = ((), (), s32[]{:S(2)}) async-start(), calls=%async_computation.8 | async-start | bytes 1327104 | tf_op jit(solution)/shard_map/all_gather | solution.py:198
  195.0 138.5 %all-gather.5.cloned.1.call-start = ((), (), s32[]{:S(2)}) async-start(), calls=%async_computation.9 | async-start | bytes 1327104 | tf_op jit(solution)/shard_map/all_gather | solution.py:199
  195.6 266.2 %all-reduce.23.cloned.1.call-start = ((), (), s32[]{:S(2)}) async-start(), calls=%async_computation.19 | async-start | bytes 12582912 | tf_op jit(solution)/shard_map/psum | solution.py:241
  324.7 137.1 %copy-start.40 = (bf16[1024,768]{1,0:T(8,128)(2,1)}, bf16[1024,768]{1,0:T(8,128)(2,1)S(1)}, u32[]{:S(2)}) copy-start(bf16[1024,768]{1,0:T(8,128)(2,1)S(1)} %get-tuple-element.1173) | copy-start | bytes 4718596
  341.6 268.0 %all-reduce.21.cloned.1.call-start = ((), (), s32[]{:S(2)}) async-start(), calls=%async_computation.18 | async-start | bytes 12582912 | tf_op jit(solution)/shard_map/psum | solution.py:259
  479.0 7.3 copy-start.103
  489.4 312.8 %reduce-scatter.35.cloned.1.call-start = ((), (), s32[]{:S(2)}) async-start(), calls=%async_computation.17 | async-start | bytes 884736
  609.6 7.4 copy-start.59
  627.4 176.5 %reduce-scatter.25.cloned.1.call-start = ((), (), s32[]{:S(2)}) async-start(), calls=%async_computation.12 | async-start | bytes 1966080
  628.8 46.3 %copy-start.9 = (bf16[1024,3,64]{0,2,1:T(8,128)(2,1)S(1)}, bf16[1024,3,64]{0,2,1:T(8,128)(2,1)}, u32[]{:S(2)}) copy-start(bf16[1024,3,64]{0,2,1:T(8,128)(2,1)} %copy-done.8) | copy-start | bytes 1179652
  628.8 7.2 copy-start.28
  650.4 6.6 copy-start.10
  650.5 7.3 copy-start.28
  675.3 7.7 copy-start.26
  695.3 7.7 copy-start.26
  724.0 81.1 %reduce-scatter.27.cloned.1.call-start = ((), (), s32[]{:S(2)}) async-start(), calls=%async_computation.13 | async-start | bytes 1966080
  727.8 122.2 %reduce-scatter.33.cloned.1.call-start = ((), (), s32[]{:S(2)}) async-start(), calls=%async_computation.16 | async-start | bytes 884736
  733.6 181.8 %reduce-scatter.31.cloned.1.call-start = ((), (), s32[]{:S(2)}) async-start(), calls=%async_computation.15 | async-start | bytes 884736
  738.7 242.4 %reduce-scatter.29.cloned.1.call-start = ((), (), s32[]{:S(2)}) async-start(), calls=%async_computation.14 | async-start | bytes 884736
  743.8 309.3 %reduce-scatter.23.cloned.1.call-start = ((), (), s32[]{:S(2)}) async-start(), calls=%async_computation.11 | async-start | bytes 2654208 | tf_op jit(solution)/shard_map/reduce_scatter | solution.py:323
  750.9 374.4 %reduce-scatter.21.cloned.1.call-start = ((), (), s32[]{:S(2)}) async-start(), calls=%async_computation.10 | async-start | bytes 2654208 | tf_op jit(solution)/shard_map/reduce_scatter | solution.py:322
  (107 other events, 360.2 us)
Sparse Core Ops, SparseCore 0:
  194.5 120.7 all-reduce.24
  341.7 119.9 all-reduce.22
  489.6 119.9 all-reduce.20
Sparse Core Ops, SparseCore 1:
  197.1 42.1 all-gather.2
  241.3 40.2 all-gather.4
  627.5 62.7 reduce-scatter.34
  724.1 28.2 reduce-scatter.24
  755.0 28.1 reduce-scatter.26
  787.4 62.6 reduce-scatter.32
  853.7 61.6 reduce-scatter.30
  919.5 61.5 reduce-scatter.28
  985.0 68.0 reduce-scatter.22
  1057.2 68.0 reduce-scatter.20
where the time goes:
time: 1140 us; the launch traced here: 1130 us
  waiting for transfers between devices  633 us (56%)
  blocking collectives  202 us (18%)
  matrix products  137 us (12%)
  other arithmetic  89.8 us (8%)
  local copies, waits for them, and re-layouts  43.1 us (4%)
  between operations  19.9 us (2%)
    unnamed x19, waiting for transfers between devices  171 us
    psum x1, waiting for transfers between devices, on_device(): lax.psum(contract_cols(expanded_low, full_up), 'tensor') + second_grad  120 us
    psum x1, waiting for transfers between devices, on_device(): lowered = lax.psum(matmul(hidden, full_down), 'tensor') + down_bias  120 us
    psum x1, waiting for transfers between devices, on_device(): attended = lax.psum(matmul(context, full_out), 'tensor') + out_bias  78.9 us
    reduce_scatter x1, waiting for transfers between devices, on_device(): lax.psum_scatter(totals[9], 'dp', scatter_dimension=0, tiled=True)  72.1 us
    reduce_scatter x1, waiting for transfers between devices, on_device(): lax.psum_scatter(totals[11], 'dp', scatter_dimension=1, tiled=True)  72 us
    unnamed x1, blocking collectives  38 us
    psum x1, blocking collectives, on_device(): bias_sums = lax.psum((totals[1], totals[4], totals[10]), 'dp')  37.7 us
  transfers between devices with their start and end apart: 13, of which 8 were waited for; matrix products, arithmetic and copies ran while one was open for 14% of the time, Pallas kernels for 0%

commit v1 on v0

--- a/solution.py
+++ b/solution.py
@@ -194,7 +194,9 @@
             lax.all_gather(owned[0], "dp", axis=0, tiled=True),
             lax.all_gather(owned[1], "dp", axis=0, tiled=True),
             lax.all_gather(owned[2], "dp", axis=0, tiled=True),
-            lax.all_gather(owned[3], "dp", axis=1, tiled=True),
+            jnp.concatenate(
+                lax.all_to_all(jnp.stack([owned[3]] * lax.axis_size("dp")), "dp", 0, 0), axis=1
+            ),
             lax.all_gather(owned[4], "dp", axis=0, tiled=True),
             lax.all_gather(owned[5], "dp", axis=1, tiled=True),
             lax.all_gather(owned[6], "dp", axis=0, tiled=True),

time: 1140 us -> 1120 us (0.982)
  blocking collectives: 202 us -> 170 us
    all_gather x1 -> x0, blocking collectives: 31.2 us -> none  [on_device(): lax.all_gather(owned[3], 'dp', axis=1, tiled=True)]
    unnamed x214 -> x211, local copies, waits for them, and re-layouts: 28.8 us -> 28.7 us
  transfers between devices with their start and end apart: 13 -> 14, of which waited for: 8 -> 8; matrix products, arithmetic and copies ran while one was open for 14% -> 19% of each run, Pallas kernels for 0% -> 0%
where the time goes in v1:
time: 1120 us; the launch traced here: 1110 us
  waiting for transfers between devices  634 us (57%)
  blocking collectives  170 us (15%)
  matrix products  137 us (12%)
  other arithmetic  90 us (8%)
  local copies, waits for them, and re-layouts  46.6 us (4%)
  between operations  19.7 us (2%)
    unnamed x19, waiting for transfers between devices  171 us
    psum x1, waiting for transfers between devices, on_device(): lowered = lax.psum(matmul(hidden, full_down), 'tensor') + down_bias  120 us
    psum x1, waiting for transfers between devices, on_device(): lax.psum(contract_cols(expanded_low, full_up), 'tensor') + second_grad  120 us
    psum x1, waiting for transfers between devices, on_device(): attended = lax.psum(matmul(context, full_out), 'tensor') + out_bias  79.6 us
    reduce_scatter x1, waiting for transfers between devices, on_device(): lax.psum_scatter(totals[9], 'dp', scatter_dimension=0, tiled=True)  72.1 us
    reduce_scatter x1, waiting for transfers between devices, on_device(): lax.psum_scatter(totals[11], 'dp', scatter_dimension=1, tiled=True)  72 us
    psum x1, blocking collectives, on_device(): bias_sums = lax.psum((totals[1], totals[4], totals[10]), 'dp')  37.7 us
    all_gather x1, blocking collectives, on_device(): lax.all_gather(owned[0], 'dp', axis=0, tiled=True)  35.9 us
  transfers between devices with their start and end apart: 14, of which 8 were waited for; matrix products, arithmetic and copies ran while one was open for 19% of the time, Pallas kernels for 0%

profile of v1, /device:TPU:0, one launch (start us, length us, event | category | flops | bytes accessed | tf_op | source)
XLA Modules:
  0.0 1112.3 jit_solution(1171593190797217667)
XLA Ops:
  9.8 7.3 all-to-all-start
  17.1 35.9 %all_gather.44 = bf16[768,192]{1,0:T(8,128)(2,1)S(1)} all-gather(bf16[96,192]{1,0:T(8,128)(2,1)} %param.30), channel_id=1, replica_groups=mesh['dp'=8,'tensor'=4] {'dp'}, dimensions={0}, use_global_device_ids=true | all-gather | bytes 331776 | tf_op jit(solution)/shard_map/all_gather | solution.py:194
  58.0 31.3 %all_gather.46 = bf16[768,192]{1,0:T(8,128)(2,1)S(1)} all-gather(bf16[96,192]{1,0:T(8,128)(2,1)S(1)} %copy-done.68), channel_id=1, replica_groups=mesh['dp'=8,'tensor'=4] {'dp'}, dimensions={0}, use_global_device_ids=true | all-gather | bytes 331776 | tf_op jit(solution)/shard_map/all_gather | solution.py:196
  91.4 31.3 %all_gather.45 = bf16[768,192]{1,0:T(8,128)(2,1)S(1)} all-gather(bf16[96,192]{1,0:T(8,128)(2,1)S(1)} %copy-done.69), channel_id=1, replica_groups=mesh['dp'=8,'tensor'=4] {'dp'}, dimensions={0}, use_global_device_ids=true | all-gather | bytes 331776 | tf_op jit(solution)/shard_map/all_gather | solution.py:195
  126.4 21.5 %while.66 = (s32[]{:T(128)}, bf16[2,512,3,64]{1,3,2,0:T(8,128)(2,1)S(1)}, f32[2,3,512]{2,1,0:T(4,128)S(1)}, s32[]{:T(128)}, s32[]{:T(128)}, /*index=5*/s32[2]{0:...) while((s32[]{:T(128)}, ...), condition=%wide.region_3.4_spmd, body=%wide.region_0.3_spmd.sunk | while | flops 419015680 | bytes 22240444 | solution.py:78
  149.0 21.0 %while.67 = (s32[]{:T(128)}, bf16[2,512,3,64]{1,3,2,0:T(8,128)(2,1)S(1)}, f32[2,3,512]{2,1,0:T(4,128)S(1)}, s32[]{:T(128)}, s32[]{:T(128)}, /*index=5*/s32[2]{0:...) while((s32[]{:T(128)}, ...), condition=%wide.region_13.14_spmd, body=%wide.region_10.13_spmd.sunk | while | flops 419015680 | bytes 22240444 | solution.py:78
  181.5 33.5 %all-reduce.16 = (bf16[768]{0:T(1024)(128)(2,1)S(1)}, bf16[768]{0:T(1024)(128)(2,1)S(1)}, bf16[768]{0:T(1024)(128)(2,1)S(1)}, bf16[768]{0:T(1024)(128)(2,1)S(1)}...) all-reduce(bf16[768]{0:T(1024)(128)(2,1)S(1)} %dynamic-update-slice, ...), channel_id=1, replica_groups=mesh['dp'=8,'tensor'=4] {'dp'}, use_global_device_ids=true, to_apply=%add | all-reduce | flops 4608 | bytes 18432
  215.1 79.6 %all-reduce.25.cloned.1.call-done = (f32[1024,768]{1,0:T(8,128)}, f32[1024,768]{1,0:T(8,128)}) async-done(((f32[1024,768]{1,0:T(8,128)}, f32[1024,768]{1,0:T(8,128)}), (f32[1024,768]{1,0:T(8,128)}, f32[1024,768]{1,0:T(8,128)})) %all-reduce.25.cloned.1.call-update) | async-done | bytes 6291472 | tf_op jit(solution)/shard_map/psum | solution.py:235
  294.6 4.7 fusion.169
  308.9 3.8 multiply_convert_fusion.3
  312.8 4.9 fusion.179
  320.9 120.1 %all-reduce.23.cloned.1.call-done = (f32[1024,768]{1,0:T(8,128)}, f32[1024,768]{1,0:T(8,128)}) async-done(((f32[1024,768]{1,0:T(8,128)}, f32[1024,768]{1,0:T(8,128)}), (f32[1024,768]{1,0:T(8,128)}, f32[1024,768]{1,0:T(8,128)})) %all-reduce.23.cloned.1.call-update) | async-done | bytes 6291472 | tf_op jit(solution)/shard_map/psum | solution.py:243
  441.0 4.2 fusion.167
  447.1 3.9 convert_reduce_fusion
  451.0 4.5 fusion.161
  468.9 120.0 %all-reduce.21.cloned.1.call-done = (f32[1024,768]{1,0:T(8,128)}, f32[1024,768]{1,0:T(8,128)}) async-done(((f32[1024,768]{1,0:T(8,128)}, f32[1024,768]{1,0:T(8,128)}), (f32[1024,768]{1,0:T(8,128)}, f32[1024,768]{1,0:T(8,128)})) %all-reduce.21.cloned.1.call-update) | async-done | bytes 6291472 | tf_op jit(solution)/shard_map/psum | solution.py:261
  589.0 5.4 multiply_reduce_fusion.3
  596.4 3.6 fusion.166
  608.2 44.5 %while.68 = (s32[]{:T(128)}, f32[1024,3,64]{0,2,1:T(8,128)}, f32[1024,3,64]{0,2,1:T(8,128)}, f32[2,512,3,64]{1,3,2,0:T(8,128)}, bf16[2,512,3,64]{1,3,2,0:T(8,128...) while((s32[]{:T(128)}, f32[1024,3,64]{0,2,1:T(8,128)}, ...), condition=%wide.region_27.28_spmd.clone, body=%wide.region_25.27_spmd.clone.sunk | while | flops 1028402176 | bytes 118828048 | solution.py:121
  615.9 3.7 multiply_reduce_fusion.16
  637.7 3.6 multiply_reduce_fusion.16
  648.9 3.7 fusion.327
  655.0 40.5 %while.69 = (s32[]{:T(128)}, f32[1024,3,64]{0,2,1:T(8,128)}, f32[1024,3,64]{0,2,1:T(8,128)}, f32[2,512,3,64]{1,3,2,0:T(8,128)}, bf16[2,512,3,64]{1,3,2,0:T(8,128...) while((s32[]{:T(128)}, f32[1024,3,64]{0,2,1:T(8,128)}, ...), condition=%wide.region_36.37_spmd.clone, body=%wide.region_34.36_spmd.clone.sunk | while | flops 1028402176 | bytes 114159056 | solution.py:121
  691.9 3.6 fusion.343
  723.6 4.0 fusion.143
  730.7 3.5 fusion.139
  740.8 37.7 %all-reduce.12 = (f32[192]{0:T(256)}, f32[192]{0:T(256)}, f32[768]{0:T(1024)S(1)}, f32[768]{0:T(1024)S(1)}, f32[768]{0:T(1024)S(1)}, /*index=5*/f32[768]{0:T(102...) all-reduce(f32[192]{0:T(256)S(1)} %add.515, ...), channel_id=1, replica_groups=mesh['dp'=8,'tensor'=4] {'dp'}, use_global_device_ids=true, to_apply=%region_41.42 | all-reduce | flops 5760 | bytes 46080 | tf_op jit(solution)/shard_map/psum | solution.py:333
  791.5 38.3 %reduce-scatter.33.cloned.1.call-done = f32[96,192]{1,0:T(8,128)} async-done(((f32[768,192]{1,0:T(8,128)}), f32[96,192]{1,0:T(8,128)}) %reduce-scatter.33.cloned.1.call-update) | async-done | bytes 73744
  829.8 65.4 %reduce-scatter.31.cloned.1.call-done = f32[96,192]{1,0:T(8,128)} async-done(((f32[768,192]{1,0:T(8,128)}), f32[96,192]{1,0:T(8,128)}) %reduce-scatter.31.cloned.1.call-update) | async-done | bytes 73744
  895.1 65.8 %reduce-scatter.29.cloned.1.call-done = f32[96,192]{1,0:T(8,128)} async-done(((f32[768,192]{1,0:T(8,128)}), f32[96,192]{1,0:T(8,128)}) %reduce-scatter.29.cloned.1.call-update) | async-done | bytes 73744
  960.9 72.0 %reduce-scatter.23.cloned.1.call-done = f32[768,96]{0,1:T(8,128)} async-done(((f32[768,768]{0,1:T(8,128)}), f32[768,96]{0,1:T(8,128)}) %reduce-scatter.23.cloned.1.call-update) | async-done | bytes 294928 | tf_op jit(solution)/shard_map/reduce_scatter | solution.py:325
  1032.9 72.1 %reduce-scatter.21.cloned.1.call-done = f32[96,768]{1,0:T(8,128)} async-done(((f32[768,768]{1,0:T(8,128)}), f32[96,768]{1,0:T(8,128)}) %reduce-scatter.21.cloned.1.call-update) | async-done | bytes 294928 | tf_op jit(solution)/shard_map/reduce_scatter | solution.py:324
  (514 shorter events, 218.3 us)
Async XLA Ops:
  8.0 48.6 %copy-start.23 = (bf16[2048,768]{1,0:T(8,128)(2,1)S(1)}, bf16[2048,768]{1,0:T(8,128)(2,1)}, u32[]{:S(2)}) copy-start(bf16[2048,768]{1,0:T(8,128)(2,1)} %param.27) | copy-start | bytes 9437188
  9.8 161.2 %all-to-all-start = ((bf16[8,192,96]{2,1,0:T(8,128)(2,1)}), bf16[8,192,96]{2,1,0:T(8,128)(2,1)}, u32[]{:S(2)}, u32[]{:S(2)}) async-start(bf16[8,192,96]{2,1,0:T(8,128)(2,1)} %stack.2), calls=%async_computation | async-start | bytes 786432 | tf_op jit(solution)/shard_map/all_to_all | solution.py:198
  17.0 277.6 %all-reduce.25.cloned.1.call-start = ((), (), s32[]{:S(2)}) async-start(), calls=%async_computation.21 | async-start | bytes 12582912 | tf_op jit(solution)/shard_map/psum | solution.py:235
  53.7 35.6 %copy-start.92 = (bf16[192]{0:T(256)(128)(2,1)S(1)}, bf16[192]{0:T(256)(128)(2,1)}, u32[]{:S(2)}) copy-start(bf16[192]{0:T(256)(128)(2,1)} %param.34) | copy-start | bytes 1156
  58.0 33.4 %copy-start.69 = (bf16[96,192]{1,0:T(8,128)(2,1)S(1)}, bf16[96,192]{1,0:T(8,128)(2,1)}, u32[]{:S(2)}) copy-start(bf16[96,192]{1,0:T(8,128)(2,1)} %param.32) | copy-start | bytes 110596
  89.3 34.2 %copy-start.43 = (bf16[768,192]{1,0:T(8,128)(2,1)}, bf16[768,192]{1,0:T(8,128)(2,1)S(1)}, u32[]{:S(2)}) copy-start(bf16[768,192]{1,0:T(8,128)(2,1)S(1)} %all_gather.46) | copy-start | bytes 884740
  89.3 33.5 %copy-start.24 = (bf16[2048,768]{1,0:T(8,128)(2,1)S(1)}, bf16[2048,768]{1,0:T(8,128)(2,1)}, u32[]{:S(2)}) copy-start(bf16[2048,768]{1,0:T(8,128)(2,1)} %param.27) | copy-start | bytes 9437188
  91.4 32.8 %copy-start.64 = (bf16[1024,192]{0,1:T(8,128)(2,1)S(1)}, bf16[1024,192]{0,1:T(8,128)(2,1)}, u32[]{:S(2)}) copy-start(bf16[1024,192]{0,1:T(8,128)(2,1)} %fusion.122) | copy-start | bytes 1179652
  126.4 21.5 %copy-start.63 = (bf16[1024,192]{0,1:T(8,128)(2,1)S(1)}, bf16[1024,192]{0,1:T(8,128)(2,1)}, u32[]{:S(2)}) copy-start(bf16[1024,192]{0,1:T(8,128)(2,1)} %fusion.123) | copy-start | bytes 1179652
  177.4 37.7 %copy-start.84 = (bf16[768]{0:T(1024)(128)(2,1)S(1)}, bf16[768]{0:T(1024)(128)(2,1)}, u32[]{:S(2)}) copy-start(bf16[768]{0:T(1024)(128)(2,1)} %param.40) | copy-start | bytes 4612
  177.4 126.6 %all-gather.3.cloned.1.call-start = ((), (), s32[]{:S(2)}) async-start(), calls=%async_computation.9 | async-start | bytes 1327104 | tf_op jit(solution)/shard_map/all_gather | solution.py:200
  178.0 134.8 %all-gather.5.cloned.1.call-start = ((), (), s32[]{:S(2)}) async-start(), calls=%async_computation.10 | async-start | bytes 1327104 | tf_op jit(solution)/shard_map/all_gather | solution.py:201
  178.6 262.4 %all-reduce.23.cloned.1.call-start = ((), (), s32[]{:S(2)}) async-start(), calls=%async_computation.20 | async-start | bytes 12582912 | tf_op jit(solution)/shard_map/psum | solution.py:243
  304.0 137.0 %copy-start.40 = (bf16[1024,768]{1,0:T(8,128)(2,1)}, bf16[1024,768]{1,0:T(8,128)(2,1)S(1)}, u32[]{:S(2)}) copy-start(bf16[1024,768]{1,0:T(8,128)(2,1)S(1)} %get-tuple-element.1173) | copy-start | bytes 4718596
  320.8 268.1 %all-reduce.21.cloned.1.call-start = ((), (), s32[]{:S(2)}) async-start(), calls=%async_computation.19 | async-start | bytes 12582912 | tf_op jit(solution)/shard_map/psum | solution.py:261
  458.4 7.3 copy-start.102
  468.8 313.2 %reduce-scatter.35.cloned.1.call-start = ((), (), s32[]{:S(2)}) async-start(), calls=%async_computation.18 | async-start | bytes 884736
  589.0 7.4 copy-start.59
  606.8 176.9 %reduce-scatter.25.cloned.1.call-start = ((), (), s32[]{:S(2)}) async-start(), calls=%async_computation.13 | async-start | bytes 1966080
  608.2 46.8 %copy-start.9 = (bf16[1024,3,64]{0,2,1:T(8,128)(2,1)S(1)}, bf16[1024,3,64]{0,2,1:T(8,128)(2,1)}, u32[]{:S(2)}) copy-start(bf16[1024,3,64]{0,2,1:T(8,128)(2,1)} %copy-done.8) | copy-start | bytes 1179652
  608.6 7.3 copy-start.28
  630.3 6.6 copy-start.10
  630.3 6.6 copy-start.21
  630.3 7.4 copy-start.28
  655.2 7.7 copy-start.26
  675.0 7.7 copy-start.26
  703.8 81.1 %reduce-scatter.27.cloned.1.call-start = ((), (), s32[]{:S(2)}) async-start(), calls=%async_computation.14 | async-start | bytes 1966080
  707.6 122.2 %reduce-scatter.33.cloned.1.call-start = ((), (), s32[]{:S(2)}) async-start(), calls=%async_computation.17 | async-start | bytes 884736
  713.4 181.8 %reduce-scatter.31.cloned.1.call-start = ((), (), s32[]{:S(2)}) async-start(), calls=%async_computation.16 | async-start | bytes 884736
  718.5 242.4 %reduce-scatter.29.cloned.1.call-start = ((), (), s32[]{:S(2)}) async-start(), calls=%async_computation.15 | async-start | bytes 884736
  723.6 309.3 %reduce-scatter.23.cloned.1.call-start = ((), (), s32[]{:S(2)}) async-start(), calls=%async_computation.12 | async-start | bytes 2654208 | tf_op jit(solution)/shard_map/reduce_scatter | solution.py:325
  730.6 374.3 %reduce-scatter.21.cloned.1.call-start = ((), (), s32[]{:S(2)}) async-start(), calls=%async_computation.11 | async-start | bytes 2654208 | tf_op jit(solution)/shard_map/reduce_scatter | solution.py:324
  (107 other events, 364.7 us)
Sparse Core Ops, SparseCore 0:
  177.5 117.0 all-reduce.24
  320.9 119.9 all-reduce.22
  469.0 119.9 all-reduce.20
Sparse Core Ops, SparseCore 1:
  180.1 38.4 all-gather.2
  220.6 40.1 all-gather.4
  606.9 62.7 reduce-scatter.34
  703.9 28.3 reduce-scatter.24
  734.8 28.1 reduce-scatter.26
  767.2 62.5 reduce-scatter.32
  833.5 61.6 reduce-scatter.30
  899.2 61.6 reduce-scatter.28
  964.8 68.0 reduce-scatter.22
  1037.0 67.9 reduce-scatter.20
